TPU v7x, 32 devices: a whole 2x2x4 slice. The times are simulated.
32 devices in a mesh: space: 8 (over y, x, core), sample: 4 (over z).
Axes of the slice: x: 2, y: 2, z: 4, core: 2. Of those that a mesh axis runs over, the one named last changes fastest.
Arguments:
- fields: bfloat16 [4, 64, 20, 8192], P('sample', 'space'), may hold values from -6 to 6
- cotangent: bfloat16 [4, 64, 20, 8192], P('sample', 'space'), may hold values from -6 to 6
- spectral_weight: bfloat16 [2, 20, 20, 4608], P(None, None, None, 'space'), may hold values from -6 to 6
- point_weight: bfloat16 [20, 20], replicated, may hold values from -1.25 to 1.25
- point_bias: float32 [20], replicated, may hold values from -1 to 1
Outputs:
- activated: bfloat16 [4, 64, 20, 8192], P('sample', 'space')
- grad_input: bfloat16 [4, 64, 20, 8192], P('sample', 'space')
- grad_spectral: float32 [2, 20, 20, 4608], P(None, None, None, ('space', 'sample'))
All inputs are finite; a program needn't handle non-finite values.
Results may differ from a plain program's by a relative error of at most 0.001.
Values sent between devices are 32-bit elements; how exact they have to be, the bound alone decides.
A program may use at most 128 MiB of HBM per device.

v0:
```python
import math

import jax
import jax.numpy as jnp
import numpy as np
from jax import lax
from jax.experimental import pallas as pl
from jax.experimental.pallas import tpu as pltpu
from jax.sharding import PartitionSpec as P

NX, NY, NZ, NT = 64, 64, 32, 4
MX, MY, MZ, MT = 12, 12, 8, 4
VOLUME = NX * NY * NZ * NT
PLANE = NZ * NT
XY = MX * MY
BF16, F32 = jnp.bfloat16, jnp.float32
VMEM_LIMIT = 60 * 1024 * 1024


def signed(modes):
    index = np.arange(modes)
    return np.where(index < modes // 2, index, index - modes)


def split_np(table):
    high = table.astype(np.float32).astype(BF16)
    low = (table - high.astype(np.float64)).astype(np.float32).astype(BF16)
    return high, low


def tables(rows, space):
    y, x = np.arange(NY)[:, None], np.arange(rows)[None, :]
    fy, fx = signed(MY)[:, None], signed(MX)[None, :]
    phi = 2 * np.pi * (
        fy.reshape(MY, 1, 1, 1) * y.reshape(1, 1, NY, 1) / NY
        + fx.reshape(1, MX, 1, 1) * x.reshape(1, 1, 1, rows) / NX
    ).reshape(XY, NY * rows)
    plane = np.concatenate([np.cos(phi), np.sin(phi)], 0)
    hi, lo = split_np(plane)
    forward = np.concatenate([hi, lo], 0)
    inverse = np.concatenate([hi.T, lo.T], 0)
    fz, ft = signed(MZ), signed(MT)
    z, t = np.arange(NZ), np.arange(NT)
    psi = 2 * np.pi * (
        fz.reshape(MZ, 1, 1, 1) * z.reshape(1, 1, NZ, 1) / NZ
        + ft.reshape(1, MT, 1, 1) * t.reshape(1, 1, 1, NT) / NT
    ).reshape(space, MZ * MT // space, PLANE)
    cos, sin = np.cos(psi), np.sin(psi)
    depth = np.stack(
        [np.concatenate([cos, -sin], -1), np.concatenate([-sin, -cos], -1)], 1
    ).reshape(MZ * 2 * MT, 2 * PLANE)
    dhi, dlo = split_np(depth)
    depth_forward = np.concatenate([dhi, dlo], 0)
    depth_inverse = np.concatenate([dhi, dhi, dlo], 0)
    return forward, inverse, depth_forward, depth_inverse


def split(value):
    high = value.astype(BF16)
    return high, (value - high.astype(F32)).astype(BF16)


def dot(a, b):
    return lax.dot_general(a, b, (((1,), (0,)), ((), ())), preferred_element_type=F32)


def forward_transform(src, fwd, depth, zhi, zlo, out, exact):
    channels = src.shape[0]
    half = fwd.shape[0] // 2

    def pair(g, carry):
        block = jnp.concatenate([src[2 * g], src[2 * g + 1]], -1)
        if exact:
            res = dot(fwd[...], block.astype(BF16))
            res = res[:half] + res[half:]
        else:
            high, low = split(block)
            res = dot(fwd[...], high)
            res = res[:half] + res[half:] + dot(fwd[:half], low)
        for k in range(2):
            part = res[:, k * PLANE : (k + 1) * PLANE]
            high, low = split(jnp.concatenate([part[:XY], part[XY:]], -1))
            zhi[2 * g + k] = high
            zlo[2 * g + k] = low
        return carry

    lax.fori_loop(0, channels // 2, pair, 0)
    rows = out.shape[0]
    contract = (((1,), (1,)), ((), ()))
    high = zhi[...].reshape(channels * XY, 2 * PLANE)
    low = zlo[...].reshape(channels * XY, 2 * PLANE)
    first = lax.dot_general(depth[...], high, contract, preferred_element_type=F32)
    second = lax.dot_general(depth[:rows], low, contract, preferred_element_type=F32)
    out[...] = first[:rows] + first[rows:] + second


def inverse_transform(modes, depth, inv, ghi, glo, dst):
    outputs = dst.shape[0]
    cells = inv.shape[0] // 2
    high, low = split(modes[...])
    stacked = jnp.concatenate([high, low, high], 0)
    lines = lax.dot_general(
        stacked, depth[...], (((0,), (0,)), ((), ())), preferred_element_type=F32
    )
    high, low = split(lines.reshape(outputs, XY, 2 * PLANE))
    ghi[:, :XY] = high[:, :, :PLANE]
    ghi[:, XY:] = high[:, :, PLANE:]
    glo[:, :XY] = low[:, :, :PLANE]
    glo[:, XY:] = low[:, :, PLANE:]

    def pair(g, carry):
        high = jnp.concatenate([ghi[2 * g], ghi[2 * g + 1]], -1)
        low = jnp.concatenate([glo[2 * g], glo[2 * g + 1]], -1)
        res = dot(inv[...], high)
        res = res[:cells] + res[cells:] + dot(inv[:cells], low)
        dst[2 * g] = res[:, :PLANE]
        dst[2 * g + 1] = res[:, PLANE:]
        return carry

    lax.fori_loop(0, outputs // 2, pair, 0)


def first_kernel(fields, fwd, depth, out, src, zhi, zlo):
    rows = fields.shape[1]

    def line(i, carry):
        at = pl.multiple_of(i * PLANE, PLANE)
        to = pl.multiple_of(i * rows, rows)
        src[:, pl.ds(to, rows), :] = fields[:, :, pl.ds(at, PLANE)].astype(F32)
        return carry

    lax.fori_loop(0, NY, line, 0)
    forward_transform(src, fwd, depth, zhi, zlo, out, True)


def middle_kernel(
    modes, fields, cot, mix, mix_back, bias, fwd, inv, depth, depth_inv,
    activated, local, out, work, ghi, glo, zhi, zlo,
):
    channels, rows, _ = fields.shape
    inverse_transform(modes, depth_inv, inv, ghi, glo, work)
    flat = channels * rows

    def line(i, carry):
        at = pl.multiple_of(i * 2 * PLANE, 2 * PLANE)
        block = fields[:, :, pl.ds(at, 2 * PLANE)].astype(F32)
        near = dot(mix[...], block.reshape(flat, 2 * PLANE).astype(BF16))
        ups = []
        for k in range(2):
            here = pl.multiple_of(at + k * PLANE, PLANE)
            to = pl.multiple_of((2 * i + k) * rows, rows)
            far = work[:, pl.ds(to, rows), :].reshape(flat, PLANE)
            pre = far + near[:, k * PLANE : (k + 1) * PLANE] + bias[...]
            phi = 0.5 * (1.0 + lax.erf(pre * (1.0 / math.sqrt(2.0))))
            slope = phi + pre * jnp.exp(-0.5 * pre * pre) * (1.0 / math.sqrt(2.0 * math.pi))
            act = (pre * phi).reshape(channels, rows, PLANE)
            activated[:, :, pl.ds(here, PLANE)] = act.astype(BF16)
            c = cot[:, :, pl.ds(here, PLANE)].astype(F32).reshape(flat, PLANE)
            up = c * slope
            work[:, pl.ds(to, rows), :] = up.reshape(channels, rows, PLANE)
            ups.append(up)
        high, low = split(jnp.concatenate(ups, -1))
        back = dot(mix_back[...], high) + dot(mix_back[...], low)
        local[:, :, pl.ds(at, 2 * PLANE)] = back.reshape(channels, rows, 2 * PLANE)
        return carry

    lax.fori_loop(0, NY // 2, line, 0)
    forward_transform(work, fwd, depth, zhi, zlo, out, False)


def last_kernel(modes, local, inv, depth_inv, out, work, ghi, glo):
    rows = local.shape[1]
    inverse_transform(modes, depth_inv, inv, ghi, glo, work)

    def line(i, carry):
        at = pl.multiple_of(i * PLANE, PLANE)
        to = pl.multiple_of(i * rows, rows)
        value = work[:, pl.ds(to, rows), :] + local[:, :, pl.ds(at, PLANE)]
        out[:, :, pl.ds(at, PLANE)] = value.astype(BF16)
        return carry

    lax.fori_loop(0, NY, line, 0)


def call(body, outs, scratch):
    return pl.pallas_call(
        body,
        out_shape=outs,
        scratch_shapes=scratch,
        compiler_params=pltpu.CompilerParams(vmem_limit_bytes=VMEM_LIMIT),
    )


def shards(fields, cotangent, spectral_weight, point_weight, point_bias):
    _, rows, channels, columns = fields.shape
    space = lax.axis_size("space")
    samples = lax.axis_size("sample")
    fwd, inv, depth, depth_inv = [jnp.asarray(t) for t in tables(rows, space)]
    owned = MT * MZ // space
    own_rows = 2 * owned
    all_rows = 2 * MT * MZ
    lanes = channels * XY
    cells = NY * rows
    field = jnp.transpose(fields[0], (1, 0, 2))
    cot = jnp.transpose(cotangent[0], (1, 0, 2))
    eye = jnp.eye(rows, dtype=BF16)
    flat = channels * rows
    mix_back = (point_weight[:, None, :, None] * eye[None, :, None, :]).reshape(flat, flat)
    mix = (point_weight.T[:, None, :, None] * eye[None, :, None, :]).reshape(flat, flat)
    bias = jnp.broadcast_to(point_bias[:, None, None], (channels, rows, PLANE)).reshape(flat, PLANE)

    freq = np.tile(signed(MX), MY * channels)
    angle = 2 * np.pi * (freq[None, :] * np.arange(space)[:, None] * rows % NX) / NX
    turn_cos = np.cos(angle).astype(np.float32)
    turn_sin = np.sin(angle).astype(np.float32)

    z_buf = pltpu.VMEM((channels, XY, 2 * PLANE), BF16)
    g_buf = pltpu.VMEM((channels, 2 * XY, PLANE), BF16)
    w_buf = pltpu.VMEM((channels, cells, PLANE), F32)
    part = jax.ShapeDtypeStruct((all_rows, lanes), F32)
    grid_bf = jax.ShapeDtypeStruct((channels, rows, columns), BF16)
    grid_f = jax.ShapeDtypeStruct((channels, rows, columns), F32)

    def to_owner(partial):
        got = lax.all_to_all(
            partial.reshape(space, own_rows, lanes), "space", 0, 0, tiled=True
        ).reshape(space, 2, owned, lanes)
        cos, sin = turn_cos[:, None, :], turn_sin[:, None, :]
        real, imag = got[:, 0], got[:, 1]
        out_r = jnp.sum(real * cos + imag * sin, 0)
        out_i = jnp.sum(imag * cos - real * sin, 0)
        both = jnp.stack([out_r, out_i]).reshape(2, owned, channels, XY)
        return jnp.transpose(both, (0, 2, 1, 3)).reshape(2, channels, -1)

    me = lax.axis_index("space")
    my_cos = lax.dynamic_slice_in_dim(jnp.asarray(turn_cos), me, 1, 0)
    my_sin = lax.dynamic_slice_in_dim(jnp.asarray(turn_sin), me, 1, 0)

    def to_slab(real, imag, scale):
        both = jnp.stack([real, imag]).reshape(2, channels, owned, XY)
        send = jnp.transpose(both, (0, 2, 1, 3)).reshape(own_rows, lanes)
        got = lax.all_to_all(
            jnp.broadcast_to(send[None], (space, own_rows, lanes)), "space", 0, 0, tiled=True
        ).reshape(space, 2, owned, lanes)
        cos, sin = my_cos * scale, my_sin * scale
        out_r = got[:, 0] * cos - got[:, 1] * sin
        out_i = got[:, 0] * sin + got[:, 1] * cos
        return jnp.stack([out_r, out_i], 1).reshape(all_rows, lanes)

    weights = spectral_weight.astype(F32)
    w_r, w_i = weights[0], weights[1]

    partial = call(first_kernel, part, [w_buf, z_buf, z_buf])(field, fwd, depth)
    s_r, s_i = to_owner(partial)
    mixed_r = jnp.sum(w_r * s_r[:, None] - w_i * s_i[:, None], 0)
    mixed_i = jnp.sum(w_r * s_i[:, None] + w_i * s_r[:, None], 0)
    modes = to_slab(mixed_r, mixed_i, 1.0 / VOLUME)
    activated, local, partial_up = call(
        middle_kernel, (grid_bf, grid_f, part), [w_buf, g_buf, g_buf, z_buf, z_buf]
    )(modes, field, cot, mix, mix_back, bias, fwd, inv, depth, depth_inv)
    u_r, u_i = to_owner(partial_up)
    u_r, u_i = u_r * (1.0 / VOLUME), u_i * (1.0 / VOLUME)
    back_r = jnp.sum(w_r * u_r[None] + w_i * u_i[None], 1)
    back_i = jnp.sum(w_r * u_i[None] - w_i * u_r[None], 1)
    modes_back = to_slab(back_r, back_i, 1.0)
    grad_input = call(last_kernel, grid_bf, [w_buf, g_buf, g_buf])(
        modes_back, local, inv, depth_inv
    )

    factors = jnp.stack([s_r, s_i, u_r, u_i]).reshape(4 * channels, samples, -1)
    factors = jnp.transpose(factors, (1, 0, 2))
    factors = lax.all_to_all(factors, "sample", 0, 0, tiled=True)
    factors = factors.reshape(samples, 4, channels, -1)
    a_r, a_i = factors[:, 0, :, None], factors[:, 1, :, None]
    b_r, b_i = factors[:, 2, None], factors[:, 3, None]
    grad_r = sum(a_r[s] * b_r[s] + a_i[s] * b_i[s] for s in range(samples))
    grad_i = sum(a_r[s] * b_i[s] - a_i[s] * b_r[s] for s in range(samples))
    grad_spectral = jnp.stack([grad_r, grad_i])
    back_to = lambda value: jnp.transpose(value, (1, 0, 2))[None]
    return back_to(activated), back_to(grad_input), grad_spectral


def solution(mesh):
    return jax.shard_map(
        shards,
        mesh=mesh,
        in_specs=(
            P("sample", "space", None, None),
            P("sample", "space", None, None),
            P(None, None, None, "space"),
            P(),
            P(),
        ),
        out_specs=(
            P("sample", "space", None, None),
            P("sample", "space", None, None),
            P(None, None, None, ("space", "sample")),
        ),
        check_vma=False,
    )
```

profile of v0, /device:TPU:0, one launch (start us, length us, event | category | flops | bytes accessed | tf_op | source)
XLA Modules:
  0.0 145.7 jit_solution(1050974316054048335)
XLA Ops:
  0.6 8.0 %shard_map.166 = f32[64,2880]{1,0:T(8,128)} custom-call(bf16[20,8,8192]{2,1,0:T(8,128)(2,1)} %bitcast.131, bf16[576,512]{1,0:T(8,128)(2,1)} %constant.31.clone.fwd, bf16[128,256]{1,0:T(8,128)(2,1)} %constant.33.clone.depth), custom_call_target="tpu_custom_call" | custom-call | tf_op jit(solution)/shard_map/pallas_call | solution.py:253
  8.6 5.2 %all-to-all-start = ((f32[8,8,2880]{2,1,0:T(8,128)}), f32[8,8,2880]{2,1,0:T(8,128)S(1)}, u32[]{:S(2)}, u32[]{:S(2)}) async-start(f32[8,8,2880]{2,1,0:T(8,128)} %bitcast.133), calls=%async_computation | async-start | bytes 1507328 | tf_op jit(solution)/shard_map/all_to_all | solution.py:225
  13.8 1.4 copy_convert_fusion
  15.2 10.8 %all-to-all-done = f32[8,8,2880]{2,1,0:T(8,128)S(1)} async-done(((f32[8,8,2880]{2,1,0:T(8,128)}), f32[8,8,2880]{2,1,0:T(8,128)S(1)}, u32[]{:S(2)}, u32[]{:S(2)}) %all-to-all-start) | async-done | bytes 737312 | tf_op jit(solution)/shard_map/all_to_all | solution.py:225
  26.0 1.1 reshape.248
  27.1 1.4 add_reduce_fusion.3
  29.0 0.4 subtract_reduce_fusion.1
  29.9 0.9 broadcast_in_dim.19
  30.8 4.2 %all-to-all-start.1 = ((f32[8,8,2880]{2,1,0:T(8,128)}), f32[8,8,2880]{2,1,0:T(8,128)}, u32[]{:S(2)}, u32[]{:S(2)}) async-start(f32[8,8,2880]{2,1,0:T(8,128)} %broadcast_in_dim.19), calls=%async_computation.1 | async-start | bytes 1507328 | tf_op jit(solution)/shard_map/all_to_all | solution.py:242
  35.2 0.7 broadcast_in_dim.21
  35.9 1.1 broadcast_multiply_fusion
  37.0 2.4 %mul.622.mix_back = bf16[160,160]{1,0:T(8,128)(2,1)} reshape(bf16[20,8,20,8]{3,2,1,0:T(8,128)(2,1)} %get-tuple-element.47) | data formatting | bytes 102400 | tf_op jit(solution)/shard_map/mul | solution.py:208
  39.4 1.2 mul.619.mix
  40.6 1.7 %dynamic-slice_reduce_fusion = (f32[2880]{0:T(1024)S(1)}, f32[2880]{0:T(1024)S(1)}, f32[2880]{0:T(1024)S(1)}, f32[2880]{0:T(1024)}) fusion(f32[8,2880]{1,0:T(8,128)} %constant.36.clone, s32[]{:T(128)S(6)} %select_n.4, f32[8,2880]{1,0:T(8,128)} %constant.35.clone), kind=kLoop, calls=%fused_computation.49 | loop fusion | flops 5760 | bytes 69124 | tf_op jit(solution)/shard_map/dynamic_slice | solution.py:237
  42.3 4.9 %all-to-all-done.1 = f32[8,8,2880]{2,1,0:T(8,128)} async-done(((f32[8,8,2880]{2,1,0:T(8,128)}), f32[8,8,2880]{2,1,0:T(8,128)}, u32[]{:S(2)}, u32[]{:S(2)}) %all-to-all-start.1) | async-done | bytes 737312 | tf_op jit(solution)/shard_map/all_to_all | solution.py:242
  47.2 1.3 reshape.249
  48.5 0.2 multiply_subtract_fusion.1
  48.7 0.2 pad_maximum_fusion.1
  48.9 1.1 reshape.250.modes
  50.0 0.7 broadcast_in_dim.22.bias
  50.7 30.7 %shard_map.167 = (bf16[20,8,8192]{2,1,0:T(8,128)(2,1)}, f32[20,8,8192]{2,1,0:T(8,128)}, f32[64,2880]{1,0:T(8,128)}) custom-call(f32[64,2880]{1,0:T(8,128)} %reshape.250.modes, bf16[20,8,8192]{2,1,0:T(8,128)(2,1)} %bitcast.132, bf16[20,8,8192]{2,1,0:T(8,128)(2,1)} %bitcast.135, bf16[160,160]{1,0:T(8,128)(2,1)} %mul.619.mix, bf16[160,160]{1,0:T(8,128)(2,1)} %mul.622.mix_back, ...), custom_call_target="tpu_custom_call" | custom-call | tf_op jit(solution)/shard_map/pallas_call | solution.py:258
  81.5 3.7 %all-to-all-start.2 = ((f32[8,8,2880]{2,1,0:T(8,128)}), f32[8,8,2880]{2,1,0:T(8,128)S(1)}, u32[]{:S(2)}, u32[]{:S(2)}) async-start(f32[8,8,2880]{2,1,0:T(8,128)} %bitcast.138), calls=%async_computation.2 | async-start | bytes 1507328 | tf_op jit(solution)/shard_map/all_to_all | solution.py:225
  85.2 0.7 copy.62
  85.8 0.7 copy.63
  86.5 1.0 unstack.22
  87.5 1.0 unstack.23
  88.6 8.7 %all-to-all-done.2 = f32[8,8,2880]{2,1,0:T(8,128)S(1)} async-done(((f32[8,8,2880]{2,1,0:T(8,128)}), f32[8,8,2880]{2,1,0:T(8,128)S(1)}, u32[]{:S(2)}, u32[]{:S(2)}) %all-to-all-start.2) | async-done | bytes 737312 | tf_op jit(solution)/shard_map/all_to_all | solution.py:225
  97.3 1.1 reshape.252
  98.3 1.4 add_reduce_fusion.2
  100.2 0.1 mul.649
  100.7 0.2 pad_maximum_fusion.3
  100.9 0.3 reshape.255
  101.2 0.9 copy.67
  102.1 4.9 %all-to-all-start.4 = ((f32[4,80,144]{1,2,0:T(8,128)}), f32[4,80,144]{1,2,0:T(8,128)S(1)}, u32[]{:S(2)}, u32[]{:S(2)}) async-start(f32[4,80,144]{1,2,0:T(8,128)} %copy.67), calls=%async_computation.4 | async-start | bytes 589824 | tf_op jit(solution)/shard_map/all_to_all | solution.py:272
  107.0 0.5 add_reduce_fusion
  107.9 6.1 %all-to-all-done.4 = f32[4,80,144]{1,2,0:T(8,128)S(1)} async-done(((f32[4,80,144]{1,2,0:T(8,128)}), f32[4,80,144]{1,2,0:T(8,128)S(1)}, u32[]{:S(2)}, u32[]{:S(2)}) %all-to-all-start.4) | async-done | bytes 184352 | tf_op jit(solution)/shard_map/all_to_all | solution.py:272
  114.0 0.9 broadcast_in_dim.25
  114.9 4.6 %all-to-all-start.3 = ((f32[8,8,2880]{2,1,0:T(8,128)}), f32[8,8,2880]{2,1,0:T(8,128)S(1)}, u32[]{:S(2)}, u32[]{:S(2)}) async-start(f32[8,8,2880]{2,1,0:T(8,128)} %broadcast_in_dim.25), calls=%async_computation.3 | async-start | bytes 1507328 | tf_op jit(solution)/shard_map/all_to_all | solution.py:242
  119.6 0.2 copy.68
  119.8 0.2 fusion.3
  120.2 3.2 %add_add_fusion = (f32[1,20,20,144]{3,0,2,1:T(1,128)S(1)}, f32[1,20,20,144]{3,0,2,1:T(1,128)S(1)}) fusion(f32[20,144]{1,0:T(8,128)S(1)} %bitcast.140, f32[20,144]{1,0:T(8,128)S(1)} %bitcast.141, f32[20,144]{1,0:T(8,128)S(1)} %bitcast.142, f32[20,144]{1,0:T(8,128)S(1)} %bitcast.143, f32[20,144]{1,0:T(8,128)S(1)} %bitcast.144, f32[20,144]{1,0:T(8,128)S(1)} %bitcast.145, ...), kind=kLoop, calls=%fused_computation.13 | loop fusion | flops 1728000 | bytes 645120 | tf_op jit(solution)/shard_map/add | solution.py:276
  123.5 1.7 %pad_maximum_fusion = f32[2,20,20,144]{3,0,2,1:T(2,128)} fusion(f32[1,20,20,144]{3,0,2,1:T(1,128)S(1)} %get-tuple-element.26, f32[1,20,20,144]{3,0,2,1:T(1,128)S(1)} %get-tuple-element.25), kind=kLoop, calls=%fused_computation.7 | loop fusion | flops 115200 | bytes 921600 | tf_op jit(solution)/shard_map/stack | solution.py:278
  125.2 6.5 %all-to-all-done.3 = f32[8,8,2880]{2,1,0:T(8,128)S(1)} async-done(((f32[8,8,2880]{2,1,0:T(8,128)}), f32[8,8,2880]{2,1,0:T(8,128)S(1)}, u32[]{:S(2)}, u32[]{:S(2)}) %all-to-all-start.3) | async-done | bytes 737312 | tf_op jit(solution)/shard_map/all_to_all | solution.py:242
  131.7 0.2 reshape.253
  132.0 0.2 multiply_subtract_fusion
  132.1 0.2 pad_maximum_fusion.2
  132.3 1.2 reshape.254.modes
  133.5 12.2 %shard_map.168 = bf16[20,8,8192]{2,1,0:T(8,128)(2,1)} custom-call(f32[64,2880]{1,0:T(8,128)} %reshape.254.modes, f32[20,8,8192]{2,1,0:T(8,128)} %get-tuple-element.8.local, bf16[1024,288]{1,0:T(8,128)(2,1)} %constant.32.clone.inv, bf16[192,256]{1,0:T(8,128)(2,1)} %constant.34.clone.depth_inv), custom_call_target="tpu_custom_call" | custom-call | tf_op jit(solution)/shard_map/pallas_call | solution.py:266
  (69 shorter events, 2.4 us)
Async XLA Ops:
  8.6 17.4 %all-to-all-start = ((f32[8,8,2880]{2,1,0:T(8,128)}), f32[8,8,2880]{2,1,0:T(8,128)S(1)}, u32[]{:S(2)}, u32[]{:S(2)}) async-start(f32[8,8,2880]{2,1,0:T(8,128)} %bitcast.133), calls=%async_computation | async-start | bytes 1507328 | tf_op jit(solution)/shard_map/all_to_all | solution.py:225
  15.2 11.9 %copy-start.2 = (f32[8,2880]{1,0:T(8,128)S(1)}, f32[8,2880]{1,0:T(8,128)}, u32[]{:S(2)}) copy-start(f32[8,2880]{1,0:T(8,128)} %constant.36.clone) | copy-start | bytes 276484
  15.2 11.9 %copy-start.4 = (f32[8,2880]{1,0:T(8,128)S(1)}, f32[8,2880]{1,0:T(8,128)}, u32[]{:S(2)}) copy-start(f32[8,2880]{1,0:T(8,128)} %constant.35.clone) | copy-start | bytes 276484
  28.7 0.7 copy-start
  29.9 5.2 %copy-start.7 = (bf16[20,20]{1,0:T(8,128)(2,1)S(1)}, bf16[20,20]{1,0:T(8,128)(2,1)}, u32[]{:S(2)}) copy-start(bf16[20,20]{1,0:T(8,128)(2,1)} %param.18) | copy-start | bytes 2404
  29.9 5.3 %copy-start.9 = (f32[20]{0:T(128)S(1)}, f32[20]{0:T(128)}, u32[]{:S(2)}) copy-start(f32[20]{0:T(128)} %param.19) | copy-start | bytes 244
  30.8 16.4 %all-to-all-start.1 = ((f32[8,8,2880]{2,1,0:T(8,128)}), f32[8,8,2880]{2,1,0:T(8,128)}, u32[]{:S(2)}, u32[]{:S(2)}) async-start(f32[8,8,2880]{2,1,0:T(8,128)} %broadcast_in_dim.19), calls=%async_computation.1 | async-start | bytes 1507328 | tf_op jit(solution)/shard_map/all_to_all | solution.py:242
  48.7 1.3 copy-start.8
  81.5 3.7 %copy-start.1 = (f32[1,20,4,144]{3,1,2,0:T(8,128)S(1)}, f32[1,20,4,144]{3,1,2,0:T(8,128)}, u32[]{:S(2)}) copy-start(f32[1,20,4,144]{3,1,2,0:T(8,128)} %copy-done) | copy-start | bytes 138244
  81.5 15.8 %all-to-all-start.2 = ((f32[8,8,2880]{2,1,0:T(8,128)}), f32[8,8,2880]{2,1,0:T(8,128)S(1)}, u32[]{:S(2)}, u32[]{:S(2)}) async-start(f32[8,8,2880]{2,1,0:T(8,128)} %bitcast.138), calls=%async_computation.2 | async-start | bytes 1507328 | tf_op jit(solution)/shard_map/all_to_all | solution.py:225
  85.2 13.2 %copy-start.3 = (f32[8,2880]{1,0:T(8,128)S(1)}, f32[8,2880]{1,0:T(8,128)}, u32[]{:S(2)}) copy-start(f32[8,2880]{1,0:T(8,128)} %constant.36.clone) | copy-start | bytes 276484
  85.8 12.5 %copy-start.5 = (f32[8,2880]{1,0:T(8,128)S(1)}, f32[8,2880]{1,0:T(8,128)}, u32[]{:S(2)}) copy-start(f32[8,2880]{1,0:T(8,128)} %constant.35.clone) | copy-start | bytes 276484
  102.1 11.9 %all-to-all-start.4 = ((f32[4,80,144]{1,2,0:T(8,128)}), f32[4,80,144]{1,2,0:T(8,128)S(1)}, u32[]{:S(2)}, u32[]{:S(2)}) async-start(f32[4,80,144]{1,2,0:T(8,128)} %copy.67), calls=%async_computation.4 | async-start | bytes 589824 | tf_op jit(solution)/shard_map/all_to_all | solution.py:272
  114.9 16.8 %all-to-all-start.3 = ((f32[8,8,2880]{2,1,0:T(8,128)}), f32[8,8,2880]{2,1,0:T(8,128)S(1)}, u32[]{:S(2)}, u32[]{:S(2)}) async-start(f32[8,8,2880]{2,1,0:T(8,128)} %broadcast_in_dim.25), calls=%async_computation.3 | async-start | bytes 1507328 | tf_op jit(solution)/shard_map/all_to_all | solution.py:242
  123.5 8.5 %copy-start.6 = (f32[2880]{0:T(1024)S(1)}, f32[2880]{0:T(1024)}, u32[]{:S(2)}) copy-start(f32[2880]{0:T(1024)} %get-tuple-element.50) | copy-start | bytes 34564
where the time goes:
time: 146 us
  Pallas kernels  50.9 us (35%)
  waiting for transfers between devices  37 us (25%)
  starting transfers between devices  22.6 us (15%)
  local copies, waits for them, and re-layouts  20.2 us (14%)
  other arithmetic  13.8 us (9%)
    pallas_call x1, Pallas kernels, shards(): call(middle_kernel, (grid_bf, grid_f, part), [w_buf, g_buf, g_buf, z_buf,...  30.7 us
    all_to_all x2, waiting for transfers between devices, to_owner(): lax.all_to_all(partial.reshape(space, own_rows, lanes), 'space', 0, 0, ti...  19.4 us
    pallas_call x1, Pallas kernels, shards(): call(last_kernel, grid_bf, [w_buf, g_buf, g_buf])  12.2 us
    all_to_all x2, waiting for transfers between devices, to_slab(): lax.all_to_all(jnp.broadcast_to(send[None], (space, own_rows, lanes)), 's...  11.5 us
    all_to_all x2, starting transfers between devices, to_owner(): lax.all_to_all(partial.reshape(space, own_rows, lanes), 'space', 0, 0, ti...  8.87 us
    all_to_all x2, starting transfers between devices, to_slab(): lax.all_to_all(jnp.broadcast_to(send[None], (space, own_rows, lanes)), 's...  8.83 us
    pallas_call x1, Pallas kernels, shards(): partial = call(first_kernel, part, [w_buf, z_buf, z_buf])(field, fwd, depth)  7.97 us
    all_to_all x1, waiting for transfers between devices, shards(): factors = lax.all_to_all(factors, 'sample', 0, 0, tiled=True)  6.07 us
  transfers between devices with their start and end apart: 5, of which 5 were waited for; matrix products, arithmetic and copies ran while one was open for 13% of the time, Pallas kernels for 0%

commit v1 on v0

--- a/solution.py
+++ b/solution.py
@@ -1,3 +1,4 @@
+import functools
 import math
 
 import jax
@@ -191,6 +192,148 @@
     )
 
 
+def swap(value):
+    half = value.shape[0] // 2
+    return jnp.concatenate([value[half:], value[:half]], 0)
+
+
+def exchange_kernel(n, ns, backward, scale_in, scale_out, *refs):
+    if backward:
+        (partial, weight, cos, sin, spec_in, modes, spec, spec_all, up_all,
+         recv, tiled, mixed, gat, s_got, u_got,
+         send_a, recv_a, send_b, recv_b, send_s, recv_s, send_u, recv_u) = refs
+    else:
+        (partial, weight, cos, sin, modes, spec,
+         recv, tiled, mixed, gat, send_a, recv_a, send_b, recv_b) = refs
+    channels, rows, lanes = weight.shape
+    width = lanes // channels
+    me = lax.axis_index("space")
+    mine = lax.axis_index("sample")
+
+    barrier = pltpu.get_barrier_semaphore()
+    for k in range(1, n):
+        pl.semaphore_signal(
+            barrier, inc=1, device_id={"space": lax.rem(me + k, n)},
+            device_id_type=pl.DeviceIdType.MESH,
+        )
+    if backward:
+        for k in range(1, ns):
+            pl.semaphore_signal(
+                barrier, inc=1, device_id={"sample": lax.rem(mine + k, ns)},
+                device_id_type=pl.DeviceIdType.MESH,
+            )
+    pl.semaphore_wait(barrier, n - 1 + (ns - 1 if backward else 0))
+
+    def start(src, dst, send, got, k, axis, target):
+        copy = pltpu.make_async_remote_copy(
+            src_ref=src, dst_ref=dst.at[k], send_sem=send.at[k], recv_sem=got.at[k],
+            device_id={axis: target}, device_id_type=pl.DeviceIdType.MESH,
+        )
+        copy.start()
+        return copy
+
+    first = []
+    for k in range(1, n):
+        target = lax.rem(me + k, n)
+        first.append(start(partial.at[target], recv, send_a, recv_a, k, "space", target))
+    side = []
+    if backward:
+        for k in range(1, ns):
+            target = lax.rem(mine + k, ns)
+            side.append(start(spec_in, s_got, send_s, recv_s, k, "sample", target))
+
+    row = lax.broadcasted_iota(jnp.int32, (rows, lanes), 0)
+    top = row < rows // 2
+    total = None
+    for k in range(n):
+        source = lax.rem(me + n - k, n)
+        if k:
+            first[k - 1].wait()
+        value = recv[k] if k else partial[me]
+        c, s = cos[pl.ds(source, 1), :], sin[pl.ds(source, 1), :]
+        turned = swap(value) * s
+        term = value * c + jnp.where(top, turned, -turned)
+        total = term if total is None else total + term
+    total = total * scale_in
+    spec[...] = total
+    if backward:
+        for k in range(1, ns):
+            target = lax.rem(mine + k, ns)
+            side.append(start(spec, u_got, send_u, recv_u, k, "sample", target))
+
+    block = tiled.shape[2]
+    for c in range(channels):
+        piece = total[:, c * width : (c + 1) * width]
+        tiled[c] = jnp.concatenate([piece] * (block // width), -1)
+    for at in range(0, lanes, block):
+        size = min(block, lanes - at)
+
+        def add(c, carry, at=at, size=size):
+            w, t = weight[c, :, at : at + size], tiled[c, :, :size]
+            return carry[0] + w * t, carry[1] + w * swap(t)
+
+        zero = jnp.zeros((rows, size), F32)
+        a, b = lax.fori_loop(0, channels, add, (zero, zero))
+        half = rows // 2
+        if backward:
+            real, imag = a[:half] + a[half:], b[:half] - b[half:]
+        else:
+            real, imag = a[:half] - a[half:], b[:half] + b[half:]
+        mixed[:, at : at + size] = jnp.concatenate([real, imag], 0)
+
+    second = []
+    for k in range(1, n):
+        target = lax.rem(me + k, n)
+        second.append(start(mixed, gat, send_b, recv_b, k, "space", target))
+    c, s = cos[pl.ds(me, 1), :] * scale_out, sin[pl.ds(me, 1), :] * scale_out
+    signed_s = jnp.where(top, -s, s)
+    for k in range(n):
+        source = lax.rem(me + n - k, n)
+        if k:
+            second[k - 1].wait()
+        value = gat[k] if k else mixed[...]
+        modes[source] = value * c + swap(value) * signed_s
+    if backward:
+        for copy in side:
+            copy.wait()
+        spec_all[mine] = spec_in[...]
+        up_all[mine] = spec[...]
+        for k in range(1, ns):
+            source = lax.rem(mine + ns - k, ns)
+            spec_all[source] = s_got[k]
+            up_all[source] = u_got[k]
+
+
+def exchange(partial, weight, cos, sin, spec_in, n, ns, scale_in, scale_out):
+    backward = spec_in is not None
+    channels, rows, lanes = weight.shape
+    width = lanes // channels
+    block = width * 128 // math.gcd(width, 128)
+    one = jax.ShapeDtypeStruct((rows, lanes), F32)
+    many = jax.ShapeDtypeStruct((n, rows, lanes), F32)
+    outs = [many, one]
+    slot = pltpu.VMEM((n, rows, lanes), F32)
+    scratch = [slot, pltpu.VMEM((channels, rows, block), F32), pltpu.VMEM((rows, lanes), F32), slot]
+    sems = [pltpu.SemaphoreType.DMA((n,))] * 4
+    args = [partial, weight, cos, sin]
+    if backward:
+        outs += [jax.ShapeDtypeStruct((ns, rows, lanes), F32)] * 2
+        scratch += [pltpu.VMEM((ns, rows, lanes), F32)] * 2
+        sems += [pltpu.SemaphoreType.DMA((ns,))] * 4
+        args.append(spec_in)
+    vmem = pl.BlockSpec(memory_space=pltpu.VMEM)
+    return pl.pallas_call(
+        functools.partial(exchange_kernel, n, ns, backward, scale_in, scale_out),
+        out_shape=outs,
+        in_specs=[vmem] * len(args),
+        out_specs=[vmem] * len(outs),
+        scratch_shapes=scratch + sems,
+        compiler_params=pltpu.CompilerParams(
+            vmem_limit_bytes=VMEM_LIMIT, collective_id=int(backward), has_side_effects=True
+        ),
+    )(*args)
+
+
 def shards(fields, cotangent, spectral_weight, point_weight, point_bias):
     _, rows, channels, columns = fields.shape
     space = lax.axis_size("space")
@@ -221,58 +364,38 @@
     grid_bf = jax.ShapeDtypeStruct((channels, rows, columns), BF16)
     grid_f = jax.ShapeDtypeStruct((channels, rows, columns), F32)
 
-    def to_owner(partial):
-        got = lax.all_to_all(
-            partial.reshape(space, own_rows, lanes), "space", 0, 0, tiled=True
-        ).reshape(space, 2, owned, lanes)
-        cos, sin = turn_cos[:, None, :], turn_sin[:, None, :]
-        real, imag = got[:, 0], got[:, 1]
-        out_r = jnp.sum(real * cos + imag * sin, 0)
-        out_i = jnp.sum(imag * cos - real * sin, 0)
-        both = jnp.stack([out_r, out_i]).reshape(2, owned, channels, XY)
-        return jnp.transpose(both, (0, 2, 1, 3)).reshape(2, channels, -1)
-
-    me = lax.axis_index("space")
-    my_cos = lax.dynamic_slice_in_dim(jnp.asarray(turn_cos), me, 1, 0)
-    my_sin = lax.dynamic_slice_in_dim(jnp.asarray(turn_sin), me, 1, 0)
-
-    def to_slab(real, imag, scale):
-        both = jnp.stack([real, imag]).reshape(2, channels, owned, XY)
-        send = jnp.transpose(both, (0, 2, 1, 3)).reshape(own_rows, lanes)
-        got = lax.all_to_all(
-            jnp.broadcast_to(send[None], (space, own_rows, lanes)), "space", 0, 0, tiled=True
-        ).reshape(space, 2, owned, lanes)
-        cos, sin = my_cos * scale, my_sin * scale
-        out_r = got[:, 0] * cos - got[:, 1] * sin
-        out_i = got[:, 0] * sin + got[:, 1] * cos
-        return jnp.stack([out_r, out_i], 1).reshape(all_rows, lanes)
-
-    weights = spectral_weight.astype(F32)
-    w_r, w_i = weights[0], weights[1]
+    weights = spectral_weight.astype(F32).reshape(2, channels, channels, owned, XY)
+    weight_up = jnp.transpose(weights, (1, 0, 3, 2, 4)).reshape(channels, own_rows, lanes)
+    weight_back = jnp.transpose(weights, (2, 0, 3, 1, 4)).reshape(channels, own_rows, lanes)
 
     partial = call(first_kernel, part, [w_buf, z_buf, z_buf])(field, fwd, depth)
-    s_r, s_i = to_owner(partial)
-    mixed_r = jnp.sum(w_r * s_r[:, None] - w_i * s_i[:, None], 0)
-    mixed_i = jnp.sum(w_r * s_i[:, None] + w_i * s_r[:, None], 0)
-    modes = to_slab(mixed_r, mixed_i, 1.0 / VOLUME)
+    split_part = lambda value: value.reshape(space, own_rows, lanes)
+    modes, spec_in = exchange(
+        split_part(partial), weight_up, turn_cos, turn_sin, None,
+        space, samples, 1.0, 1.0 / VOLUME,
+    )
     activated, local, partial_up = call(
         middle_kernel, (grid_bf, grid_f, part), [w_buf, g_buf, g_buf, z_buf, z_buf]
-    )(modes, field, cot, mix, mix_back, bias, fwd, inv, depth, depth_inv)
-    u_r, u_i = to_owner(partial_up)
-    u_r, u_i = u_r * (1.0 / VOLUME), u_i * (1.0 / VOLUME)
-    back_r = jnp.sum(w_r * u_r[None] + w_i * u_i[None], 1)
-    back_i = jnp.sum(w_r * u_i[None] - w_i * u_r[None], 1)
-    modes_back = to_slab(back_r, back_i, 1.0)
+    )(modes.reshape(all_rows, lanes), field, cot, mix, mix_back, bias, fwd, inv, depth, depth_inv)
+    modes_back, _, spec_all, up_all = exchange(
+        split_part(partial_up), weight_back, turn_cos, turn_sin, spec_in,
+        space, samples, 1.0 / VOLUME, 1.0,
+    )
     grad_input = call(last_kernel, grid_bf, [w_buf, g_buf, g_buf])(
-        modes_back, local, inv, depth_inv
-    )
-
-    factors = jnp.stack([s_r, s_i, u_r, u_i]).reshape(4 * channels, samples, -1)
-    factors = jnp.transpose(factors, (1, 0, 2))
-    factors = lax.all_to_all(factors, "sample", 0, 0, tiled=True)
-    factors = factors.reshape(samples, 4, channels, -1)
-    a_r, a_i = factors[:, 0, :, None], factors[:, 1, :, None]
-    b_r, b_i = factors[:, 2, None], factors[:, 3, None]
+        modes_back.reshape(all_rows, lanes), local, inv, depth_inv
+    )
+
+    mine = lax.axis_index("sample")
+    count = owned * XY // samples
+
+    def own_block(value):
+        value = value.reshape(samples, 2, owned, channels, XY)
+        value = jnp.transpose(value, (0, 1, 3, 2, 4)).reshape(samples, 2, channels, owned * XY)
+        return lax.dynamic_slice_in_dim(value, mine * count, count, 3)
+
+    a, b = own_block(spec_all), own_block(up_all)
+    a_r, a_i = a[:, 0, :, None], a[:, 1, :, None]
+    b_r, b_i = b[:, 0, None], b[:, 1, None]
     grad_r = sum(a_r[s] * b_r[s] + a_i[s] * b_i[s] for s in range(samples))
     grad_i = sum(a_r[s] * b_i[s] - a_i[s] * b_r[s] for s in range(samples))
     grad_spectral = jnp.stack([grad_r, grad_i])

time: 146 us -> 139 us (0.952)
  Pallas kernels: 50.9 us -> 104 us
  waiting for transfers between devices: 37 us -> 0 us
  starting transfers between devices: 22.6 us -> 0 us
  other arithmetic: 13.8 us -> 5.17 us
  local copies, waits for them, and re-layouts: 20.2 us -> 28.3 us
    pallas_call x0 -> x2, Pallas kernels: none -> 53.1 us  [exchange(): pl.pallas_call(functools.partial(exchange_kernel, n, ns, backward, scale_...]
    all_to_all x5 -> x0, waiting for transfers between devices: 37 us -> none  [the longest x2 19.4 us: to_owner(): lax.all_to_all(partial.reshape(space, own_rows, lanes), 'space', 0, 0, ti...]
    all_to_all x5 -> x0, starting transfers between devices: 22.6 us -> none  [the longest x2 8.87 us: to_owner(): lax.all_to_all(partial.reshape(space, own_rows, lanes), 'space', 0, 0, ti...]
    reshape x7 -> x9, local copies, waits for them, and re-layouts: 6.28 us -> 22.2 us  [the longest x3 11.2 us: shards(): spectral_weight.astype(F32).reshape(2, channels, channels, owned, XY)]
    another operation x16 -> x0, local copies, waits for them, and re-layouts: 4.34 us -> none  [the longest x7 3.48 us: shards(): s_r, s_i = to_owner(partial)]
    reduce_sum x4 -> x0, other arithmetic: 3.69 us -> none  [the longest x2 2.78 us: to_owner(): out_r = jnp.sum(real * cos + imag * sin, 0)]
    broadcast_in_dim x4 -> x0, local copies, waits for them, and re-layouts: 2.07 us -> none  [to_slab(): jnp.broadcast_to(send[None], (space, own_rows, lanes))]
    dynamic_slice x1 -> x0, other arithmetic: 1.66 us -> none  [shards(): my_sin = lax.dynamic_slice_in_dim(jnp.asarray(turn_sin), me, 1, 0)]
  transfers between devices with their start and end apart: 5 -> 0, of which waited for: 5 -> 0; matrix products, arithmetic and copies ran while one was open for 13% -> 0% of each run, Pallas kernels for 0% -> 0%
where the time goes in v1:
time: 139 us; the launch traced here: 138 us
  Pallas kernels  104 us (75%)
  local copies, waits for them, and re-layouts  28.3 us (20%)
  other arithmetic  5.17 us (4%)
    pallas_call x2, Pallas kernels, exchange(): pl.pallas_call(functools.partial(exchange_kernel, n, ns, backward, scale_...  53.1 us
    pallas_call x1, Pallas kernels, shards(): call(middle_kernel, (grid_bf, grid_f, part), [w_buf, g_buf, g_buf, z_buf,...  30.7 us
    pallas_call x1, Pallas kernels, shards(): call(last_kernel, grid_bf, [w_buf, g_buf, g_buf])  12.3 us
    reshape x3, local copies, waits for them, and re-layouts, shards(): spectral_weight.astype(F32).reshape(2, channels, channels, owned, XY)  11.2 us
    pallas_call x1, Pallas kernels, shards(): partial = call(first_kernel, part, [w_buf, z_buf, z_buf])(field, fwd, depth)  7.96 us
    reshape x1, local copies, waits for them, and re-layouts, shards(): jnp.transpose(weights, (2, 0, 3, 1, 4)).reshape(channels, own_rows, lanes)  4.41 us
    reshape x1, local copies, waits for them, and re-layouts, shards(): jnp.transpose(weights, (1, 0, 3, 2, 4)).reshape(channels, own_rows, lanes)  4.39 us
    add x1, other arithmetic, shards(): grad_r = sum((a_r[s] * b_r[s] + a_i[s] * b_i[s] for s in range(samples)))  3.25 us

profile of v1, /device:TPU:0, one launch (start us, length us, event | category | flops | bytes accessed | tf_op | source)
XLA Modules:
  0.0 138.4 jit_solution(14914473465156584622)
XLA Ops:
  0.6 0.0 copy-start.2
  0.7 0.8 copy.18
  1.5 0.7 broadcast_in_dim.20
  2.2 0.1 broadcast_in_dim.21
  2.3 0.7 broadcast_in_dim.22.bias
  3.0 8.0 %shard_map.130 = f32[64,2880]{1,0:T(8,128)} custom-call(bf16[20,8,8192]{2,1,0:T(8,128)(2,1)} %bitcast.81, bf16[576,512]{1,0:T(8,128)(2,1)} %constant.22.clone.fwd, bf16[128,256]{1,0:T(8,128)(2,1)} %constant.24.clone.depth), custom_call_target="tpu_custom_call" | custom-call | tf_op jit(solution)/shard_map/pallas_call | solution.py:371
  11.0 0.0 copy-done.2
  11.0 0.2 broadcast_multiply_fusion
  11.2 1.2 mul.364.mix_back
  12.4 1.2 mul.361.mix
  13.6 4.4 %reshape.198 = f32[2,20,20,4,144]{4,3,0,2,1:T(4,128)S(1)} reshape(bf16[2,20,20,576]{3,0,2,1:T(2,128)(2,1)} %param.13) | data formatting | bytes 2764800 | tf_op jit(solution)/shard_map/reshape | solution.py:367
  18.0 3.8 %copy.56 = f32[2,20,20,4,144]{4,1,3,0,2:T(8,128)} copy(f32[2,20,20,4,144]{4,3,0,2,1:T(4,128)S(1)} %reshape.198) | data formatting | bytes 3686400 | tf_op jit(solution)/shard_map/reshape | solution.py:367
  21.8 4.4 %reshape.191.refs_1_ = f32[20,8,2880]{2,1,0:T(8,128)} reshape(f32[20,2,4,20,144]{4,3,2,1,0:T(8,128)} %bitcast.80) | data formatting | bytes 3686400 | tf_op jit(solution)/shard_map/reshape | solution.py:369
  26.2 3.0 %copy.57 = f32[2,20,20,4,144]{4,2,3,0,1:T(8,128)} copy(f32[2,20,20,4,144]{4,3,0,2,1:T(4,128)S(1)} %reshape.198) | data formatting | bytes 3686400 | tf_op jit(solution)/shard_map/reshape | solution.py:367
  29.2 4.4 %reshape.188.refs_1_ = f32[20,8,2880]{2,1,0:T(8,128)} reshape(f32[20,2,4,20,144]{4,3,2,1,0:T(8,128)} %bitcast.79) | data formatting | bytes 3686400 | tf_op jit(solution)/shard_map/reshape | solution.py:368
  33.6 25.8 %shard_map.131 = (f32[8,8,2880]{2,1,0:T(8,128)}, f32[8,2880]{1,0:T(8,128)}) custom-call(f32[8,8,2880]{2,1,0:T(8,128)} %bitcast.85, f32[20,8,2880]{2,1,0:T(8,128)} %reshape.188.refs_1_, f32[8,2880]{1,0:T(8,128)} %constant.26.clone.refs_2_, f32[8,2880]{1,0:T(8,128)} %constant.27.clone.refs_3_), custom_call_target="tpu_custom_call" | custom-call | tf_op jit(solution)/shard_map/pallas_call | solution.py:325
  59.4 30.7 %shard_map.132 = (bf16[20,8,8192]{2,1,0:T(8,128)(2,1)}, f32[20,8,8192]{2,1,0:T(8,128)}, f32[64,2880]{1,0:T(8,128)}) custom-call(f32[64,2880]{1,0:T(8,128)} %bitcast.89, bf16[20,8,8192]{2,1,0:T(8,128)(2,1)} %bitcast.82, bf16[20,8,8192]{2,1,0:T(8,128)(2,1)} %bitcast.87, bf16[160,160]{1,0:T(8,128)(2,1)} %mul.361.mix, bf16[160,160]{1,0:T(8,128)(2,1)} %mul.364.mix_back, ...), custom_call_target="tpu_custom_call" | custom-call | tf_op jit(solution)/shard_map/pallas_call | solution.py:377
  90.1 27.4 %shard_map.133 = (f32[8,8,2880]{2,1,0:T(8,128)}, f32[8,2880]{1,0:T(8,128)}, f32[4,8,2880]{2,1,0:T(8,128)}, f32[4,8,2880]{2,1,0:T(8,128)}) custom-call(f32[8,8,2880]{2,1,0:T(8,128)} %bitcast.88, f32[20,8,2880]{2,1,0:T(8,128)} %reshape.191.refs_1_, f32[8,2880]{1,0:T(8,128)} %constant.26.clone.refs_2_, f32[8,2880]{1,0:T(8,128)} %constant.27.clone.refs_3_, ...), custom_call_target="tpu_custom_call" | custom-call | tf_op jit(solution)/shard_map/pallas_call | solution.py:325
  117.5 0.0 copy-start.1
  117.5 12.3 %shard_map.134 = bf16[20,8,8192]{2,1,0:T(8,128)(2,1)} custom-call(f32[64,2880]{1,0:T(8,128)} %bitcast.90, f32[20,8,8192]{2,1,0:T(8,128)} %get-tuple-element.16.local, bf16[1024,288]{1,0:T(8,128)(2,1)} %constant.23.clone.inv, bf16[192,256]{1,0:T(8,128)(2,1)} %constant.25.clone.depth_inv), custom_call_target="tpu_custom_call" | custom-call | tf_op jit(solution)/shard_map/pallas_call | solution.py:384
  129.8 0.0 copy-start
  129.8 0.0 copy-done.1
  129.8 0.4 reshape.193
  130.2 0.3 copy.20
  130.5 0.6 reshape.194
  131.1 0.0 copy-done
  131.1 0.4 reshape.195
  131.6 0.3 copy.21
  131.8 0.6 reshape.196
  132.5 0.8 constant_dynamic-slice_fusion.12
  133.5 3.2 %add_add_fusion = (f32[1,20,20,144]{3,0,2,1:T(1,128)S(1)}, f32[1,20,20,144]{3,0,2,1:T(1,128)S(1)}) fusion(f32[20,144]{1,0:T(8,128)S(1)} %bitcast.98, f32[20,144]{1,0:T(8,128)S(1)} %bitcast.99, f32[20,144]{1,0:T(8,128)S(1)} %bitcast.92, f32[20,144]{1,0:T(8,128)S(1)} %bitcast.105, f32[20,144]{1,0:T(8,128)S(1)} %bitcast.93, f32[20,144]{1,0:T(8,128)S(1)} %bitcast.104, ...), kind=kLoop, calls=%fused_computation.6 | loop fusion | flops 1728000 | bytes 645120 | tf_op jit(solution)/shard_map/add | solution.py:399
  136.7 1.7 %pad_maximum_fusion = f32[2,20,20,144]{3,0,2,1:T(2,128)} fusion(f32[1,20,20,144]{3,0,2,1:T(1,128)S(1)} %get-tuple-element.36, f32[1,20,20,144]{3,0,2,1:T(1,128)S(1)} %get-tuple-element.35), kind=kLoop, calls=%fused_computation.2 | loop fusion | flops 115200 | bytes 921600 | tf_op jit(solution)/shard_map/stack | solution.py:401
  (17 shorter events, 0.1 us)
Async XLA Ops:
  0.6 10.4 %copy-start.2 = (bf16[20,20]{1,0:T(8,128)(2,1)S(1)}, bf16[20,20]{1,0:T(8,128)(2,1)}, u32[]{:S(2)}) copy-start(bf16[20,20]{1,0:T(8,128)(2,1)} %param.14) | copy-start | bytes 2404
  117.5 12.3 %copy-start.1 = (f32[4,8,2880]{2,1,0:T(8,128)S(1)}, f32[4,8,2880]{2,1,0:T(8,128)}, u32[]{:S(2)}) copy-start(f32[4,8,2880]{2,1,0:T(8,128)} %get-tuple-element.17) | copy-start | bytes 1105924
  129.8 1.4 copy-start

commit v2 on v1

--- a/solution.py
+++ b/solution.py
@@ -135,12 +135,21 @@
 
 
 def middle_kernel(
-    modes, fields, cot, mix, mix_back, bias, fwd, inv, depth, depth_inv,
-    activated, local, out, work, ghi, glo, zhi, zlo,
+    modes, fields, cot, point, point_t, bias_row, copies, copies_t, same, fwd, inv, depth, depth_inv,
+    activated, local, out, work, ghi, glo, zhi, zlo, mix, mix_back, bias,
 ):
     channels, rows, _ = fields.shape
     inverse_transform(modes, depth_inv, inv, ghi, glo, work)
     flat = channels * rows
+
+    def spread(matrix):
+        half = dot(copies[...], matrix).astype(BF16)
+        return dot(half, copies_t[...]).astype(BF16) * same[...]
+
+    mix_back[...] = spread(point[...])
+    mix[...] = spread(point_t[...])
+    column = jnp.sum(copies[...].astype(F32) * bias_row[...], -1, keepdims=True)
+    bias[...] = jnp.broadcast_to(column, (flat, PLANE))
 
     def line(i, carry):
         at = pl.multiple_of(i * 2 * PLANE, 2 * PLANE)
@@ -169,8 +178,9 @@
     forward_transform(work, fwd, depth, zhi, zlo, out, False)
 
 
-def last_kernel(modes, local, inv, depth_inv, out, work, ghi, glo):
+def last_kernel(modes, local, spec_all, up_all, inv, depth_inv, out, grad, work, ghi, glo):
     rows = local.shape[1]
+    samples, _, channels, count = spec_all.shape
     inverse_transform(modes, depth_inv, inv, ghi, glo, work)
 
     def line(i, carry):
@@ -181,6 +191,20 @@
         return carry
 
     lax.fori_loop(0, NY, line, 0)
+
+    def term(c, carry):
+        real = jnp.zeros((channels, count), F32)
+        imag = jnp.zeros((channels, count), F32)
+        for s in range(samples):
+            a_r, a_i = spec_all[s, 0, pl.ds(c, 1), :], spec_all[s, 1, pl.ds(c, 1), :]
+            b_r, b_i = up_all[s, 0], up_all[s, 1]
+            real = real + (a_r * b_r + a_i * b_i)
+            imag = imag + (a_r * b_i - a_i * b_r)
+        grad[c, :, 0, :] = real
+        grad[c, :, 1, :] = imag
+        return carry
+
+    lax.fori_loop(0, channels, term, 0)
 
 
 def call(body, outs, scratch):
@@ -199,14 +223,17 @@
 
 def exchange_kernel(n, ns, backward, scale_in, scale_out, *refs):
     if backward:
-        (partial, weight, cos, sin, spec_in, modes, spec, spec_all, up_all,
-         recv, tiled, mixed, gat, s_got, u_got,
+        (partial, weight, cos, sin, spec_in, modes, spec_all, up_all,
+         recv, stage, lined, out_lined, mixed, gat, s_got, u_got, spec,
          send_a, recv_a, send_b, recv_b, send_s, recv_s, send_u, recv_u) = refs
     else:
         (partial, weight, cos, sin, modes, spec,
-         recv, tiled, mixed, gat, send_a, recv_a, send_b, recv_b) = refs
-    channels, rows, lanes = weight.shape
-    width = lanes // channels
+         recv, stage, lined, out_lined, mixed, gat, send_a, recv_a, send_b, recv_b) = refs
+    _, rows, lanes = partial.shape
+    channels, width = stage.shape[0], stage.shape[2]
+    owned = rows // 2
+    per = ns // owned
+    count = width // per
     me = lax.axis_index("space")
     mine = lax.axis_index("sample")
 
@@ -240,7 +267,7 @@
     if backward:
         for k in range(1, ns):
             target = lax.rem(mine + k, ns)
-            side.append(start(spec_in, s_got, send_s, recv_s, k, "sample", target))
+            side.append(start(spec_in.at[target], s_got, send_s, recv_s, k, "sample", target))
 
     row = lax.broadcasted_iota(jnp.int32, (rows, lanes), 0)
     top = row < rows // 2
@@ -255,31 +282,45 @@
         term = value * c + jnp.where(top, turned, -turned)
         total = term if total is None else total + term
     total = total * scale_in
-    spec[...] = total
+    for c in range(channels):
+        stage[c] = total[:, c * width : (c + 1) * width]
+    for j in range(rows):
+        r, q = j // owned, j % owned
+        block = stage[:, j, :]
+        lined[r, :, q * width : (q + 1) * width] = block
+        for p in range(per):
+            spec[q * per + p, r] = block[:, p * count : (p + 1) * count]
     if backward:
         for k in range(1, ns):
             target = lax.rem(mine + k, ns)
-            side.append(start(spec, u_got, send_u, recv_u, k, "sample", target))
-
-    block = tiled.shape[2]
+            side.append(start(spec.at[target], u_got, send_u, recv_u, k, "sample", target))
+
+    if backward:
+
+        def reduce(c, carry):
+            w_r, w_i = weight[0, c], weight[1, c]
+            u_r, u_i = lined[0], lined[1]
+            out_lined[0, pl.ds(c, 1), :] = jnp.sum(w_r * u_r + w_i * u_i, 0, keepdims=True)
+            out_lined[1, pl.ds(c, 1), :] = jnp.sum(w_r * u_i - w_i * u_r, 0, keepdims=True)
+            return carry
+
+        lax.fori_loop(0, channels, reduce, 0)
+    else:
+
+        def add(c, carry):
+            w_r, w_i = weight[0, c], weight[1, c]
+            s_r, s_i = lined[0, pl.ds(c, 1), :], lined[1, pl.ds(c, 1), :]
+            return carry[0] + (w_r * s_r - w_i * s_i), carry[1] + (w_r * s_i + w_i * s_r)
+
+        zero = jnp.zeros((channels, owned * width), F32)
+        real, imag = lax.fori_loop(0, channels, add, (zero, zero))
+        out_lined[0] = real
+        out_lined[1] = imag
+    for j in range(rows):
+        r, q = j // owned, j % owned
+        stage[:, j, :] = out_lined[r, :, q * width : (q + 1) * width]
     for c in range(channels):
-        piece = total[:, c * width : (c + 1) * width]
-        tiled[c] = jnp.concatenate([piece] * (block // width), -1)
-    for at in range(0, lanes, block):
-        size = min(block, lanes - at)
-
-        def add(c, carry, at=at, size=size):
-            w, t = weight[c, :, at : at + size], tiled[c, :, :size]
-            return carry[0] + w * t, carry[1] + w * swap(t)
-
-        zero = jnp.zeros((rows, size), F32)
-        a, b = lax.fori_loop(0, channels, add, (zero, zero))
-        half = rows // 2
-        if backward:
-            real, imag = a[:half] + a[half:], b[:half] - b[half:]
-        else:
-            real, imag = a[:half] - a[half:], b[:half] + b[half:]
-        mixed[:, at : at + size] = jnp.concatenate([real, imag], 0)
+        mixed[:, c * width : (c + 1) * width] = stage[c]
 
     second = []
     for k in range(1, n):
@@ -296,29 +337,29 @@
     if backward:
         for copy in side:
             copy.wait()
-        spec_all[mine] = spec_in[...]
-        up_all[mine] = spec[...]
+        spec_all[0] = spec_in[mine]
+        up_all[0] = spec[mine]
         for k in range(1, ns):
-            source = lax.rem(mine + ns - k, ns)
-            spec_all[source] = s_got[k]
-            up_all[source] = u_got[k]
+            spec_all[k] = s_got[k]
+            up_all[k] = u_got[k]
 
 
 def exchange(partial, weight, cos, sin, spec_in, n, ns, scale_in, scale_out):
     backward = spec_in is not None
-    channels, rows, lanes = weight.shape
-    width = lanes // channels
-    block = width * 128 // math.gcd(width, 128)
-    one = jax.ShapeDtypeStruct((rows, lanes), F32)
+    _, channels, _, modes = weight.shape
+    _, rows, lanes = partial.shape
     many = jax.ShapeDtypeStruct((n, rows, lanes), F32)
-    outs = [many, one]
+    kept = (ns, 2, channels, modes // ns)
+    outs = [many] if backward else [many, jax.ShapeDtypeStruct(kept, F32)]
     slot = pltpu.VMEM((n, rows, lanes), F32)
-    scratch = [slot, pltpu.VMEM((channels, rows, block), F32), pltpu.VMEM((rows, lanes), F32), slot]
+    line = pltpu.VMEM((2, channels, modes), F32)
+    stage = pltpu.VMEM((channels, rows, lanes // channels), F32)
+    scratch = [slot, stage, line, line, pltpu.VMEM((rows, lanes), F32), slot]
     sems = [pltpu.SemaphoreType.DMA((n,))] * 4
     args = [partial, weight, cos, sin]
     if backward:
-        outs += [jax.ShapeDtypeStruct((ns, rows, lanes), F32)] * 2
-        scratch += [pltpu.VMEM((ns, rows, lanes), F32)] * 2
+        outs += [jax.ShapeDtypeStruct(kept, F32)] * 2
+        scratch += [pltpu.VMEM(kept, F32)] * 3
         sems += [pltpu.SemaphoreType.DMA((ns,))] * 4
         args.append(spec_in)
     vmem = pl.BlockSpec(memory_space=pltpu.VMEM)
@@ -346,11 +387,10 @@
     cells = NY * rows
     field = jnp.transpose(fields[0], (1, 0, 2))
     cot = jnp.transpose(cotangent[0], (1, 0, 2))
-    eye = jnp.eye(rows, dtype=BF16)
     flat = channels * rows
-    mix_back = (point_weight[:, None, :, None] * eye[None, :, None, :]).reshape(flat, flat)
-    mix = (point_weight.T[:, None, :, None] * eye[None, :, None, :]).reshape(flat, flat)
-    bias = jnp.broadcast_to(point_bias[:, None, None], (channels, rows, PLANE)).reshape(flat, PLANE)
+    copies = np.repeat(np.eye(channels), rows, 0).astype(BF16)
+    same = np.tile(np.eye(rows), (channels, channels)).astype(BF16)
+    flat_buf = pltpu.VMEM((flat, flat), BF16)
 
     freq = np.tile(signed(MX), MY * channels)
     angle = 2 * np.pi * (freq[None, :] * np.arange(space)[:, None] * rows % NX) / NX
@@ -364,41 +404,30 @@
     grid_bf = jax.ShapeDtypeStruct((channels, rows, columns), BF16)
     grid_f = jax.ShapeDtypeStruct((channels, rows, columns), F32)
 
-    weights = spectral_weight.astype(F32).reshape(2, channels, channels, owned, XY)
-    weight_up = jnp.transpose(weights, (1, 0, 3, 2, 4)).reshape(channels, own_rows, lanes)
-    weight_back = jnp.transpose(weights, (2, 0, 3, 1, 4)).reshape(channels, own_rows, lanes)
+    weights = spectral_weight.astype(F32)
 
     partial = call(first_kernel, part, [w_buf, z_buf, z_buf])(field, fwd, depth)
     split_part = lambda value: value.reshape(space, own_rows, lanes)
     modes, spec_in = exchange(
-        split_part(partial), weight_up, turn_cos, turn_sin, None,
+        split_part(partial), weights, turn_cos, turn_sin, None,
         space, samples, 1.0, 1.0 / VOLUME,
     )
     activated, local, partial_up = call(
-        middle_kernel, (grid_bf, grid_f, part), [w_buf, g_buf, g_buf, z_buf, z_buf]
-    )(modes.reshape(all_rows, lanes), field, cot, mix, mix_back, bias, fwd, inv, depth, depth_inv)
-    modes_back, _, spec_all, up_all = exchange(
-        split_part(partial_up), weight_back, turn_cos, turn_sin, spec_in,
+        middle_kernel, (grid_bf, grid_f, part), [w_buf, g_buf, g_buf, z_buf, z_buf, flat_buf, flat_buf, pltpu.VMEM((flat, PLANE), F32)]
+    )(
+        modes.reshape(all_rows, lanes), field, cot, point_weight, point_weight.T,
+        point_bias[None], copies, copies.T, same, fwd, inv, depth, depth_inv,
+    )
+    modes_back, spec_all, up_all = exchange(
+        split_part(partial_up), weights, turn_cos, turn_sin, spec_in,
         space, samples, 1.0 / VOLUME, 1.0,
     )
-    grad_input = call(last_kernel, grid_bf, [w_buf, g_buf, g_buf])(
-        modes_back.reshape(all_rows, lanes), local, inv, depth_inv
-    )
-
-    mine = lax.axis_index("sample")
     count = owned * XY // samples
-
-    def own_block(value):
-        value = value.reshape(samples, 2, owned, channels, XY)
-        value = jnp.transpose(value, (0, 1, 3, 2, 4)).reshape(samples, 2, channels, owned * XY)
-        return lax.dynamic_slice_in_dim(value, mine * count, count, 3)
-
-    a, b = own_block(spec_all), own_block(up_all)
-    a_r, a_i = a[:, 0, :, None], a[:, 1, :, None]
-    b_r, b_i = b[:, 0, None], b[:, 1, None]
-    grad_r = sum(a_r[s] * b_r[s] + a_i[s] * b_i[s] for s in range(samples))
-    grad_i = sum(a_r[s] * b_i[s] - a_i[s] * b_r[s] for s in range(samples))
-    grad_spectral = jnp.stack([grad_r, grad_i])
+    grad_shape = jax.ShapeDtypeStruct((channels, channels, 2, count), F32)
+    grad_input, grad = call(last_kernel, (grid_bf, grad_shape), [w_buf, g_buf, g_buf])(
+        modes_back.reshape(all_rows, lanes), local, spec_all, up_all, inv, depth_inv
+    )
+    grad_spectral = jnp.transpose(grad, (2, 0, 1, 3))
     back_to = lambda value: jnp.transpose(value, (1, 0, 2))[None]
     return back_to(activated), back_to(grad_input), grad_spectral
 

time: 139 us -> 111 us (0.80)
  local copies, waits for them, and re-layouts: 28.3 us -> 1.47 us
  other arithmetic: 5.17 us -> 1.6 us
  Pallas kernels: 104 us -> 106 us
    reshape x9 -> x0, local copies, waits for them, and re-layouts: 22.2 us -> none  [the longest x3 11.2 us: shards(): spectral_weight.astype(F32).reshape(2, channels, channels, owned, XY)]
    add x1 -> x0, other arithmetic: 3.25 us -> none  [shards(): grad_r = sum((a_r[s] * b_r[s] + a_i[s] * b_i[s] for s in range(samples)))]
    mul x2 -> x0, local copies, waits for them, and re-layouts: 2.35 us -> none  [the longest x1 1.17 us: shards(): point_weight[:, None, :, None] * eye[None, :, None, :]]
    another operation x1 -> x0, other arithmetic: 1.72 us -> none  [shards(): grad_spectral = jnp.stack([grad_r, grad_i])]
    convert_element_type x1, other arithmetic: 0.01 us -> 1.6 us  [shards(): weights = spectral_weight.astype(F32)]
    broadcast_in_dim x3 -> x0, local copies, waits for them, and re-layouts: 1.54 us -> none  [shards(): jnp.broadcast_to(point_bias[:, None, None], (channels, rows, PLANE))]
    unnamed x22 -> x3, local copies, waits for them, and re-layouts: 0.07 us -> 1.47 us
where the time goes in v2:
time: 111 us; the launch traced here: 110 us
  Pallas kernels  106 us (95%)
  other arithmetic  1.6 us (1%)
  local copies, waits for them, and re-layouts  1.47 us (1%)
    pallas_call x2, Pallas kernels, exchange(): pl.pallas_call(functools.partial(exchange_kernel, n, ns, backward, scale_...  53.9 us
    pallas_call x1, Pallas kernels, shards(): call(middle_kernel, (grid_bf, grid_f, part), [w_buf, g_buf, g_buf, z_buf,...  31 us
    pallas_call x1, Pallas kernels, shards(): call(last_kernel, (grid_bf, grad_shape), [w_buf, g_buf, g_buf])  13.5 us
    pallas_call x1, Pallas kernels, shards(): partial = call(first_kernel, part, [w_buf, z_buf, z_buf])(field, fwd, depth)  7.96 us

profile of v2, /device:TPU:0, one launch (start us, length us, event | category | flops | bytes accessed | tf_op | source)
XLA Modules:
  0.0 110.1 jit_solution(11532927208333207970)
XLA Ops:
  0.6 0.0 copy-start
  0.6 1.5 %copy.18 = bf16[20,20]{0,1:T(8,128)(2,1)} copy(bf16[20,20]{1,0:T(8,128)(2,1)} %point.1) | data formatting | bytes 1600 | tf_op args[3]
  2.1 8.0 %shard_map.157 = f32[64,2880]{1,0:T(8,128)} custom-call(bf16[20,8,8192]{2,1,0:T(8,128)(2,1)} %bitcast.19, bf16[576,512]{1,0:T(8,128)(2,1)} %constant.18.clone.fwd, bf16[128,256]{1,0:T(8,128)(2,1)} %constant.20.clone.depth), custom_call_target="tpu_custom_call" | custom-call | tf_op jit(solution)/shard_map/pallas_call | solution.py:409
  10.1 0.0 copy-done
  10.1 1.6 %copy_convert_fusion.refs_1_ = f32[2,20,20,576]{3,2,1,0:T(8,128)} fusion(bf16[2,20,20,576]{3,0,2,1:T(2,128)(2,1)S(1)} %copy-done), kind=kLoop, calls=%fused_computation | loop fusion | flops 460800 | bytes 2764800 | tf_op jit(solution)/shard_map/convert_element_type | solution.py:407
  11.7 26.2 %shard_map.158 = (f32[8,8,2880]{2,1,0:T(8,128)}, f32[4,2,20,144]{3,2,1,0:T(8,128)}) custom-call(f32[8,8,2880]{2,1,0:T(8,128)} %bitcast.21, f32[2,20,20,576]{3,2,1,0:T(8,128)} %copy_convert_fusion.refs_1_, f32[8,2880]{1,0:T(8,128)} %constant.22.clone.refs_2_, f32[8,2880]{1,0:T(8,128)} %constant.23.clone.refs_3_), custom_call_target="tpu_custom_call" | custom-call | tf_op jit(solution)/shard_map/pallas_call | solution.py:366
  37.9 31.0 %shard_map.159 = (bf16[20,8,8192]{2,1,0:T(8,128)(2,1)}, f32[20,8,8192]{2,1,0:T(8,128)}, f32[64,2880]{1,0:T(8,128)}) custom-call(f32[64,2880]{1,0:T(8,128)} %bitcast.25, bf16[20,8,8192]{2,1,0:T(8,128)(2,1)} %bitcast.20, bf16[20,8,8192]{2,1,0:T(8,128)(2,1)} %bitcast.22, bf16[20,20]{1,0:T(8,128)(2,1)} %point.1, bf16[20,20]{1,0:T(8,128)(2,1)} %bitcast.26, ...), custom_call_target="tpu_custom_call" | custom-call | tf_op jit(solution)/shard_map/pallas_call | solution.py:415
  68.9 27.7 %shard_map.160 = (f32[8,8,2880]{2,1,0:T(8,128)}, f32[4,2,20,144]{3,2,1,0:T(8,128)}, f32[4,2,20,144]{3,2,1,0:T(8,128)}) custom-call(f32[8,8,2880]{2,1,0:T(8,128)} %bitcast.23, f32[2,20,20,576]{3,2,1,0:T(8,128)} %copy_convert_fusion.refs_1_, f32[8,2880]{1,0:T(8,128)} %constant.22.clone.refs_2_, f32[8,2880]{1,0:T(8,128)} %constant.23.clone.refs_3_, ...), custom_call_target="tpu_custom_call" | custom-call | tf_op jit(solution)/shard_map/pallas_call | solution.py:366
  96.6 13.5 %shard_map.161 = (bf16[20,8,8192]{2,1,0:T(8,128)(2,1)}, f32[20,20,2,144]{3,2,1,0:T(2,128)}) custom-call(f32[64,2880]{1,0:T(8,128)} %bitcast.24, f32[20,8,8192]{2,1,0:T(8,128)} %get-tuple-element.18.local, f32[4,2,20,144]{3,2,1,0:T(8,128)} %get-tuple-element.19.spec_all, f32[4,2,20,144]{3,2,1,0:T(8,128)} %get-tuple-element.20.up_all, ...), custom_call_target="tpu_custom_call" | custom-call | tf_op jit(solution)/shard_map/pallas_call | solution.py:427
Async XLA Ops:
  0.6 9.4 %copy-start = (bf16[2,20,20,576]{3,0,2,1:T(2,128)(2,1)S(1)}, bf16[2,20,20,576]{3,0,2,1:T(2,128)(2,1)}, u32[]{:S(2)}) copy-start(bf16[2,20,20,576]{3,0,2,1:T(2,128)(2,1)} %param.16) | copy-start | bytes 2764804

commit v3 on v2

--- a/solution.py
+++ b/solution.py
@@ -224,11 +224,11 @@
 def exchange_kernel(n, ns, backward, scale_in, scale_out, *refs):
     if backward:
         (partial, weight, cos, sin, spec_in, modes, spec_all, up_all,
-         recv, stage, lined, out_lined, mixed, gat, s_got, u_got, spec,
-         send_a, recv_a, send_b, recv_b, send_s, recv_s, send_u, recv_u) = refs
+         recv, stage, lined, out_lined, mixed, gat, pre, joined, gat_near, s_got, u_got, spec,
+         send_a, recv_a, send_b, recv_b, send_c, recv_c, send_d, recv_d, send_s, recv_s, send_u, recv_u) = refs
     else:
         (partial, weight, cos, sin, modes, spec,
-         recv, stage, lined, out_lined, mixed, gat, send_a, recv_a, send_b, recv_b) = refs
+         recv, stage, lined, out_lined, mixed, gat, pre, joined, gat_near, send_a, recv_a, send_b, recv_b, send_c, recv_c, send_d, recv_d) = refs
     _, rows, lanes = partial.shape
     channels, width = stage.shape[0], stage.shape[2]
     owned = rows // 2
@@ -259,10 +259,11 @@
         copy.start()
         return copy
 
-    first = []
-    for k in range(1, n):
-        target = lax.rem(me + k, n)
-        first.append(start(partial.at[target], recv, send_a, recv_a, k, "space", target))
+    sibling = me + 1 - 2 * lax.rem(me, 2)
+    near = {}
+    for k in range(0, n, 2):
+        target = lax.rem(sibling + k, n)
+        near[k] = start(partial.at[target], pre, send_d, recv_d, k, "space", sibling)
     side = []
     if backward:
         for k in range(1, ns):
@@ -271,16 +272,23 @@
 
     row = lax.broadcasted_iota(jnp.int32, (rows, lanes), 0)
     top = row < rows // 2
-    total = None
-    for k in range(n):
-        source = lax.rem(me + n - k, n)
-        if k:
-            first[k - 1].wait()
-        value = recv[k] if k else partial[me]
+
+    def turn(value, source):
         c, s = cos[pl.ds(source, 1), :], sin[pl.ds(source, 1), :]
         turned = swap(value) * s
-        term = value * c + jnp.where(top, turned, -turned)
-        total = term if total is None else total + term
+        return value * c + jnp.where(top, turned, -turned)
+
+    first = {}
+    for k in list(range(2, n, 2)) + [0]:
+        near[k].wait()
+        target = lax.rem(me + k, n)
+        joined[k] = turn(partial[target], me) + turn(pre[k], sibling)
+        if k:
+            first[k] = start(joined.at[k], recv, send_a, recv_a, k, "space", target)
+    total = joined[0]
+    for k in range(2, n, 2):
+        first[k].wait()
+        total = total + recv[k]
     total = total * scale_in
     for c in range(channels):
         stage[c] = total[:, c * width : (c + 1) * width]
@@ -322,18 +330,24 @@
     for c in range(channels):
         mixed[:, c * width : (c + 1) * width] = stage[c]
 
-    second = []
-    for k in range(1, n):
-        target = lax.rem(me + k, n)
-        second.append(start(mixed, gat, send_b, recv_b, k, "space", target))
+    second, relay = {}, {}
+    for k in range(2, n, 2):
+        second[k] = start(mixed, gat, send_b, recv_b, k, "space", lax.rem(me + k, n))
+    relay[0] = start(mixed, gat_near, send_c, recv_c, 0, "space", sibling)
     c, s = cos[pl.ds(me, 1), :] * scale_out, sin[pl.ds(me, 1), :] * scale_out
     signed_s = jnp.where(top, -s, s)
-    for k in range(n):
-        source = lax.rem(me + n - k, n)
-        if k:
-            second[k - 1].wait()
-        value = gat[k] if k else mixed[...]
+
+    def place(value, source):
         modes[source] = value * c + swap(value) * signed_s
+
+    place(mixed[...], me)
+    for k in range(2, n, 2):
+        second[k].wait()
+        relay[k] = start(gat.at[k], gat_near, send_c, recv_c, k, "space", sibling)
+        place(gat[k], lax.rem(me + n - k, n))
+    for k in range(0, n, 2):
+        relay[k].wait()
+        place(gat_near[k], lax.rem(sibling + n - k, n))
     if backward:
         for copy in side:
             copy.wait()
@@ -354,8 +368,8 @@
     slot = pltpu.VMEM((n, rows, lanes), F32)
     line = pltpu.VMEM((2, channels, modes), F32)
     stage = pltpu.VMEM((channels, rows, lanes // channels), F32)
-    scratch = [slot, stage, line, line, pltpu.VMEM((rows, lanes), F32), slot]
-    sems = [pltpu.SemaphoreType.DMA((n,))] * 4
+    scratch = [slot, stage, line, line, pltpu.VMEM((rows, lanes), F32), slot, slot, slot, slot]
+    sems = [pltpu.SemaphoreType.DMA((n,))] * 8
     args = [partial, weight, cos, sin]
     if backward:
         outs += [jax.ShapeDtypeStruct(kept, F32)] * 2

time: 111 us -> 103 us (0.928)
  Pallas kernels: 106 us -> 98.7 us
    pallas_call x2, Pallas kernels: 53.9 us -> 46.2 us  [exchange(): pl.pallas_call(functools.partial(exchange_kernel, n, ns, backward, scale_...]
where the time goes in v3:
time: 103 us; the launch traced here: 102 us
  Pallas kernels  98.7 us (96%)
  other arithmetic  1.6 us (2%)
  local copies, waits for them, and re-layouts  1.47 us (1%)
    pallas_call x2, Pallas kernels, exchange(): pl.pallas_call(functools.partial(exchange_kernel, n, ns, backward, scale_...  46.2 us
    pallas_call x1, Pallas kernels, shards(): call(middle_kernel, (grid_bf, grid_f, part), [w_buf, g_buf, g_buf, z_buf,...  31 us
    pallas_call x1, Pallas kernels, shards(): call(last_kernel, (grid_bf, grad_shape), [w_buf, g_buf, g_buf])  13.5 us
    pallas_call x1, Pallas kernels, shards(): partial = call(first_kernel, part, [w_buf, z_buf, z_buf])(field, fwd, depth)  7.96 us

profile of v3, /device:TPU:0, one launch (start us, length us, event | category | flops | bytes accessed | tf_op | source)
XLA Modules:
  0.0 102.5 jit_solution(12069957796681844029)
XLA Ops:
  0.6 0.0 copy-start
  0.6 1.5 %copy.18 = bf16[20,20]{0,1:T(8,128)(2,1)} copy(bf16[20,20]{1,0:T(8,128)(2,1)} %point.1) | data formatting | bytes 1600 | tf_op args[3]
  2.1 8.0 %shard_map.157 = f32[64,2880]{1,0:T(8,128)} custom-call(bf16[20,8,8192]{2,1,0:T(8,128)(2,1)} %bitcast.19, bf16[576,512]{1,0:T(8,128)(2,1)} %constant.18.clone.fwd, bf16[128,256]{1,0:T(8,128)(2,1)} %constant.20.clone.depth), custom_call_target="tpu_custom_call" | custom-call | tf_op jit(solution)/shard_map/pallas_call | solution.py:423
  10.1 0.0 copy-done
  10.1 1.6 %copy_convert_fusion.refs_1_ = f32[2,20,20,576]{3,2,1,0:T(8,128)} fusion(bf16[2,20,20,576]{3,0,2,1:T(2,128)(2,1)S(1)} %copy-done), kind=kLoop, calls=%fused_computation | loop fusion | flops 460800 | bytes 2764800 | tf_op jit(solution)/shard_map/convert_element_type | solution.py:421
  11.7 23.0 %shard_map.158 = (f32[8,8,2880]{2,1,0:T(8,128)}, f32[4,2,20,144]{3,2,1,0:T(8,128)}) custom-call(f32[8,8,2880]{2,1,0:T(8,128)} %bitcast.21, f32[2,20,20,576]{3,2,1,0:T(8,128)} %copy_convert_fusion.refs_1_, f32[8,2880]{1,0:T(8,128)} %constant.22.clone.refs_2_, f32[8,2880]{1,0:T(8,128)} %constant.23.clone.refs_3_), custom_call_target="tpu_custom_call" | custom-call | tf_op jit(solution)/shard_map/pallas_call | solution.py:380
  34.7 31.0 %shard_map.159 = (bf16[20,8,8192]{2,1,0:T(8,128)(2,1)}, f32[20,8,8192]{2,1,0:T(8,128)}, f32[64,2880]{1,0:T(8,128)}) custom-call(f32[64,2880]{1,0:T(8,128)} %bitcast.25, bf16[20,8,8192]{2,1,0:T(8,128)(2,1)} %bitcast.20, bf16[20,8,8192]{2,1,0:T(8,128)(2,1)} %bitcast.22, bf16[20,20]{1,0:T(8,128)(2,1)} %point.1, bf16[20,20]{1,0:T(8,128)(2,1)} %bitcast.26, ...), custom_call_target="tpu_custom_call" | custom-call | tf_op jit(solution)/shard_map/pallas_call | solution.py:429
  65.7 23.3 %shard_map.160 = (f32[8,8,2880]{2,1,0:T(8,128)}, f32[4,2,20,144]{3,2,1,0:T(8,128)}, f32[4,2,20,144]{3,2,1,0:T(8,128)}) custom-call(f32[8,8,2880]{2,1,0:T(8,128)} %bitcast.23, f32[2,20,20,576]{3,2,1,0:T(8,128)} %copy_convert_fusion.refs_1_, f32[8,2880]{1,0:T(8,128)} %constant.22.clone.refs_2_, f32[8,2880]{1,0:T(8,128)} %constant.23.clone.refs_3_, ...), custom_call_target="tpu_custom_call" | custom-call | tf_op jit(solution)/shard_map/pallas_call | solution.py:380
  89.0 13.5 %shard_map.161 = (bf16[20,8,8192]{2,1,0:T(8,128)(2,1)}, f32[20,20,2,144]{3,2,1,0:T(2,128)}) custom-call(f32[64,2880]{1,0:T(8,128)} %bitcast.24, f32[20,8,8192]{2,1,0:T(8,128)} %get-tuple-element.18.local, f32[4,2,20,144]{3,2,1,0:T(8,128)} %get-tuple-element.19.spec_all, f32[4,2,20,144]{3,2,1,0:T(8,128)} %get-tuple-element.20.up_all, ...), custom_call_target="tpu_custom_call" | custom-call | tf_op jit(solution)/shard_map/pallas_call | solution.py:441
Async XLA Ops:
  0.6 9.4 %copy-start = (bf16[2,20,20,576]{3,0,2,1:T(2,128)(2,1)S(1)}, bf16[2,20,20,576]{3,0,2,1:T(2,128)(2,1)}, u32[]{:S(2)}) copy-start(bf16[2,20,20,576]{3,0,2,1:T(2,128)(2,1)} %param.16) | copy-start | bytes 2764804
